TPU v7x, 128 devices: a whole 4x4x4 slice. The times are simulated.
128 devices in a mesh: sector: 4 (over y_hi, core), owner: 32 (over x, y_lo, z).
Axes of the slice: x: 4, y: 4 (y_hi: 2, y_lo: 2; y = y_hi * 2 + y_lo), z: 4, core: 2. Of those that a mesh axis runs over, the one named last changes fastest.
Arguments:
- broadcast_ops: float32 [4, 4, 1024, 1024], P('sector', None, 'owner'), may hold values from -0.1875 to 0.1875
- resident_ops: float32 [4, 32, 1024, 1024], P('sector', 'owner'), may hold values from -6 to 6
- integrals: float32 [4, 32, 4, 4], P('sector', 'owner'), may hold values from -3 to 3
- owner_list: int32 [32, 4], P('owner'), may hold values from 0 to 3, as said below
Outputs:
- complementary: float32 [4, 32, 2, 1024, 1024], P('sector', 'owner')
Inputs may be any that keep to these rules, and one draw needn't show every extreme that they name: `owner_list`: in each row one sector group is named exactly 2 times, one is not named, and every other is named once.
All inputs are finite; a program needn't handle non-finite values.
Results may differ from a plain program's by a relative error of at most 0.012.
Values may be sent and summed in bfloat16 or wider, within the bound.
A program may use at most 64 MiB of HBM per device.

v0:
```python
import jax
import jax.numpy as jnp
from jax import lax
from jax.sharding import PartitionSpec as P

CAP = 2


def shards(broadcast_ops, resident_ops, integrals, owner_list):
    highest = lax.Precision.HIGHEST
    shared = broadcast_ops[0]
    resident = resident_ops[0, 0]
    weights = integrals[0, 0]
    owners = owner_list[0]
    pair_count = owners.shape[0]
    slot_count = CAP
    sector_id = lax.axis_index("sector")
    products = jnp.einsum(
        "krj,jn->krn",
        lax.all_gather(shared.astype(jnp.bfloat16), "owner", axis=1, tiled=True).astype(
            jnp.float32
        ),
        resident,
        precision=highest,
    )
    pair_index = jnp.arange(pair_count)
    same_owner = owners[:, None] == owners[None, :]
    earlier = pair_index[:, None] < pair_index[None, :]
    slot_rank = jnp.sum((same_owner & earlier).astype(jnp.int32), axis=0)
    partial_ops = jnp.einsum("pk,kmn->pmn", weights, products, precision=highest)
    pair_total = lax.psum(partial_ops.astype(jnp.bfloat16), "sector").astype(jnp.float32)
    selector = (
        (owners[None, :] == sector_id) & (slot_rank[None, :] == jnp.arange(slot_count)[:, None])
    ).astype(jnp.float32)
    result = jnp.einsum("cp,pmn->cmn", selector, pair_total, precision=highest)
    return result[None, None]


def solution(mesh):
    in_specs = (
        P("sector", None, "owner", None),
        P("sector", "owner", None, None),
        P("sector", "owner", None, None),
        P("owner", None),
    )
    out_specs = P("sector", "owner", None, None, None)
    return jax.shard_map(shards, mesh=mesh, in_specs=in_specs, out_specs=out_specs, check_vma=False)
```

profile of v0, /device:TPU:1, one launch (start us, length us, event | category | flops | bytes accessed | tf_op | source)
XLA Modules:
  0.0 435.2 jit_solution(6021242355717869884)
XLA Ops:
  6.5 0.0 copy-start
  6.5 0.0 all-gather.3.cloned.1.call-start
  6.5 1.8 convert_element_type.19
  8.3 0.0 all-gather.3.cloned.1.call-update
  8.4 0.0 all-reduce.2.cloned.1.call-start
  8.4 149.4 %all-gather.3.cloned.1.call-done = bf16[1,4,1024,1024]{3,2,1,0:T(8,128)(2,1)} async-done(((bf16[1,4,32,1024]{3,2,1,0:T(8,128)(2,1)}), bf16[1,4,1024,1024]{3,2,1,0:T(8,128)(2,1)}) %all-gather.3.cloned.1.call-update) | async-done | bytes 8388624 | tf_op jit(solution)/shard_map/all_gather | solution.py:20
  157.8 31.4 %fusion.2 = f32[4,1024,1024]{2,1,0:T(8,128)S(1)} fusion(bf16[1,4,1024,1024]{3,2,1,0:T(8,128)(2,1)} %all-gather.3.cloned.1.call-done, f32[1,1,1024,1024]{3,2,1,0:T(8,128)} %param.5), kind=kOutput, calls=%fused_computation.2 | convolution fusion | flops 51539607552 | bytes 29360128 | tf_op jit(solution)/shard_map/krj,jn->krn/dot_general | solution.py:18
  189.2 0.0 copy-done
  189.2 44.7 %convert_bitcast_fusion = bf16[4,1024,1024]{2,0,1:T(4,128)(2,1)} fusion(f32[4,1024,1024]{2,1,0:T(8,128)S(1)} %fusion.2, f32[1,1,4,4]{3,2,1,0:T(4,128)S(1)} %copy-done), kind=kOutput, calls=%fused_computation.4 | convolution fusion | flops 205520896 | bytes 25165888 | tf_op jit(solution)/shard_map/pk,kmn->pmn/dot_general | solution.py:30
  233.9 0.0 copy-start.1
  233.9 0.0 all-reduce.2.cloned.1.call-update
  233.9 0.6 copy-done.1
  234.6 0.1 convert_reduce_fusion
  234.7 180.7 %all-reduce.2.cloned.1.call-done = bf16[4,1024,1024]{2,0,1:T(4,128)(2,1)} async-done(((bf16[4,1024,1024]{2,0,1:T(4,128)(2,1)}), bf16[4,1024,1024]{2,0,1:T(4,128)(2,1)}) %all-reduce.2.cloned.1.call-update) | async-done | bytes 8388624 | tf_op jit(solution)/shard_map/psum | solution.py:31
  415.4 7.0 %convolution_bitcast_fusion = f32[1,1,2,1024,1024]{4,2,3,1,0:T(2,128)S(1)} fusion(bf16[4,1024,1024]{2,0,1:T(4,128)(2,1)} %all-reduce.2.cloned.1.call-done, pred[4]{0:T(512)(128)(4,1)S(1)} %compare_bitcast_fusion, s32[4]{0:T(128)S(1)} %convert_reduce_fusion), kind=kOutput, calls=%fused_computation.5 | convolution fusion | flops 16777232 | bytes 16777236 | tf_op jit(solution)/shard_map/cp,pmn->cmn/dot_general | solution.py:35
  422.4 6.0 %copy.6 = f32[1,1,2,1024,1024]{4,3,2,1,0:T(8,128)} copy(f32[1,1,2,1024,1024]{4,2,3,1,0:T(2,128)S(1)} %convolution_bitcast_fusion) | data formatting | bytes 16777216 | tf_op jit(solution)/shard_map/broadcast_in_dim | solution.py:36
  (1 shorter events, 0.0 us)
Async XLA Ops:
  6.5 182.6 %copy-start = (f32[1,1,4,4]{3,2,1,0:T(4,128)S(1)}, f32[1,1,4,4]{3,2,1,0:T(4,128)}, u32[]{:S(2)}) copy-start(f32[1,1,4,4]{3,2,1,0:T(4,128)} %param.6) | copy-start | bytes 196
  6.5 151.2 %all-gather.3.cloned.1.call-start = ((), (), s32[]{:S(2)}) async-start(), calls=%async_computation.1 | async-start | bytes 8650752 | tf_op jit(solution)/shard_map/all_gather | solution.py:20
  8.4 407.0 %all-reduce.2.cloned.1.call-start = ((), (), s32[]{:S(2)}) async-start(), calls=%async_computation | async-start | bytes 16777216 | tf_op jit(solution)/shard_map/psum | solution.py:31
  233.9 0.7 copy-start.1
Sparse Core Ops, SparseCore 0:
  9.0 148.7 all-gather.2
  234.1 181.2 all-reduce.1
where the time goes:
time: 435 us
  waiting for transfers between devices  330 us (76%)
  matrix products  83.2 us (19%)
  between operations  13.4 us (3%)
  local copies, waits for them, and re-layouts  6.59 us (2%)
    psum x1, waiting for transfers between devices, shards(): lax.psum(partial_ops.astype(jnp.bfloat16), 'sector').astype(jnp.float32)  181 us
    all_gather x1, waiting for transfers between devices, shards(): lax.all_gather(shared.astype(jnp.bfloat16), 'owner', axis=1, tiled=True)  149 us
    dot_general x1, matrix products, shards(): jnp.einsum('pk,kmn->pmn', weights, products, precision=highest)  44.7 us
    dot_general x1, matrix products, shards(): jnp.einsum('krj,jn->krn', lax.all_gather(shared.astype(jnp.bfloat16), 'ow...  31.4 us
  transfers between devices with their start and end apart: 2, of which 2 were waited for; matrix products, arithmetic and copies ran while one was open for 0% of the time, Pallas kernels for 0%

commit v1 on v0

v1 whole, which is shorter than its diff:
```python
import jax
import jax.numpy as jnp
from jax import lax
from jax.experimental import pallas as pl
from jax.experimental.pallas import tpu as pltpu
from jax.sharding import PartitionSpec as P

MESH = pl.DeviceIdType.MESH
BF = jnp.bfloat16
F32 = jnp.float32
LAG = 4


def coords():
    s = lax.axis_index("sector")
    o = lax.axis_index("owner")
    return o // 8, lax.rem(o // 4, 2), lax.rem(o, 4), s // 2, lax.rem(s, 2)


def device(x, yl, z, yh, c):
    return (yh * 2 + c, lax.rem(x, 4) * 8 + yl * 4 + lax.rem(z, 4))


def kernel(b_hbm, r_hbm, wt_hbm, out_hbm, bf32, rf32, bst, ops, res, wts, wide, give, take, own, done,
           load_sem, pair_send, pair_recv, res_send, res_recv, ag_send, ag_recv, ex_send, ex_recv,
           out_sem, fin_send, fin_recv):
    x, yl, z, yh, c = coords()
    partner = device(x, yl, z, yh, 1 - c)
    y_near = device(x, 1 - yl, z, yh, c)
    y_far = device(x, yl, z, 1 - yh, c)

    def first(r):
        return device(x + (4 - r) * (1 - c), yl, z + (4 - r) * c, yh, c)

    def second(r):
        return device(x + (4 - r) * c, yl, z + (4 - r) * (1 - c), yh, c)

    def row_of(u, v, core):
        early = (u + 12) // 16
        r1 = u * (1 - early) + ((u + 8) // 3 - 4) * early
        r2 = lax.rem(u + 8, 3) * early + early
        xs = lax.rem(x + r1 * (1 - core) + r2 * core, 4)
        zs = lax.rem(z + r1 * core + r2 * (1 - core), 4)
        ys = yl * (1 - v) + (1 - yl) * v
        return pl.multiple_of((xs * 8 + ys * 4 + zs) * 32 + core * 16, 16)

    def remote(src, dst, ssem, rsem, dev):
        return pltpu.make_async_remote_copy(
            src_ref=src, dst_ref=dst, send_sem=ssem, recv_sem=rsem, device_id=dev, device_id_type=MESH
        )

    load_b = pltpu.make_async_copy(b_hbm, bf32, load_sem.at[0])
    load_b.start()
    load_w = pltpu.make_async_copy(wt_hbm, wts.at[c], load_sem.at[1])
    load_w.start()

    def load_r(i):
        part = pl.ds(i * 256, 256)
        return pltpu.make_async_copy(r_hbm.at[part], rf32.at[part], load_sem.at[2 + i])

    for i in range(4):
        load_r(i).start()

    barrier = pltpu.get_barrier_semaphore()
    peers = [partner, y_near, y_far] + [first(r) for r in (1, 2, 3)] + [second(r) for r in (1, 2, 3)]
    for peer in peers:
        pl.semaphore_signal(barrier, inc=1, device_id=peer, device_id_type=MESH)
    pl.semaphore_wait(barrier, len(peers))

    load_b.wait()
    mine = pl.ds(pl.multiple_of(c * 16, 16), 16)
    theirs = pl.ds(pl.multiple_of((1 - c) * 16, 16), 16)
    for k in range(4):
        bst[k] = bf32[k, theirs, :].astype(BF)
    send_b = remote(bst, ops.at[0, 0, c], pair_send.at[0], ag_recv.at[0], partner)
    send_b.start()
    for k in range(4):
        ops[0, 0, c, k] = bf32[k, mine, :].astype(BF)
    load_w.wait()
    send_w = remote(wts.at[c], wts.at[c], pair_send.at[1], pair_recv.at[0], partner)
    send_w.start()

    def ag_to_first(r, v):
        return remote(ops.at[0, v], ops.at[r, v], ag_send.at[24 + v * 3 + r - 1], ag_recv.at[r * 2 + v], first(r))

    def ag_to_second(u, v, r):
        to = 4 + 3 * u + r - 1
        return remote(ops.at[u, v], ops.at[to, v], ag_send.at[(u * 2 + v) * 3 + r - 1],
                      ag_recv.at[to * 2 + v], second(r))

    def arrived(u, v):
        remote(ops.at[u, v], ops.at[u, v], ag_send.at[0], ag_recv.at[u * 2 + v], partner).wait_recv()

    remote(bst, ops.at[0, 0, 1 - c], pair_send.at[0], ag_recv.at[0], partner).wait_recv()
    ag_y = remote(ops.at[0, 0], ops.at[0, 1], ag_send.at[30], ag_recv.at[1], y_near)
    ag_y.start()
    for r in (1, 3, 2):
        ag_to_first(r, 0).start()
    for r in (1, 3, 2):
        ag_to_second(0, 0, r).start()

    def send_r(i, core):
        part = pl.ds(pl.multiple_of(core * 1024 + i * 256, 256), 256)
        return remote(res.at[part], res.at[part], res_send.at[i], res_recv.at[i], partner)

    for i in range(4):
        load_r(i).wait()
        res[pl.ds(pl.multiple_of(c * 1024 + i * 256, 256), 256), :] = rf32[i * 256:(i + 1) * 256, :].astype(BF)
        send_r(i, c).start()

    arrived(0, 1)
    for r in (1, 3, 2):
        ag_to_first(r, 1).start()
    for r in (1, 3, 2):
        ag_to_second(0, 1, r).start()

    remote(wts.at[1 - c], wts.at[1 - c], pair_send.at[1], pair_recv.at[0], partner).wait_recv()
    for i in range(4):
        send_r(i, 1 - c).wait_recv()

    def exchange(u):
        return remote(give.at[u], take.at[u], ex_send.at[u], ex_recv.at[u], y_far)

    def put_own(u, v):
        return pltpu.make_async_copy(
            done.at[u, c, :, v], out_hbm.at[:, pl.ds(row_of(u, v, c), 16), :], out_sem.at[u * 2 + v])

    def put_partner(u, v, core):
        return remote(done.at[u, 1 - c, :, v], out_hbm.at[:, pl.ds(row_of(u, v, core), 16), :],
                      fin_send.at[u * 2 + v], fin_recv.at[u * 2 + v], partner)

    @pl.loop(0, 16 + LAG)
    def _(u):
        @pl.when(u < 16)
        def _():
            @pl.when(u > 0)
            def _():
                for v in range(2):
                    arrived(u, v)

            @pl.when((u > 0) & (u < 4))
            def _():
                for v in range(2):
                    for r in (1, 3, 2):
                        ag_to_second(u, v, r).start()

            for s in range(2):
                for v in range(2):
                    for half in range(2):
                        lanes = [slice(half * 512 + i * 128, half * 512 + (i + 1) * 128) for i in range(4)]
                        b = [[ops[u, v, s, k, :, lane].astype(F32) for lane in lanes] for k in range(4)]
                        for t in range(6):
                            w = [jnp.broadcast_to(wts[s, t * 4 + k:t * 4 + k + 1, :], (16, 128)) for k in range(4)]
                            for i in range(4):
                                acc = (b[0][i] * w[0] + b[1][i] * w[1]) + (b[2][i] * w[2] + b[3][i] * w[3])
                                col = s * 1024 + half * 512 + i * 128
                                wide[t * 32 + v * 16:t * 32 + v * 16 + 16, col:col + 128] = acc.astype(BF)
            for n in range(4):
                cols = slice(n * 256, (n + 1) * 256)
                part = jnp.dot(wide[...], res[:, cols], preferred_element_type=F32)
                give[u, :, cols] = part[:96].astype(BF)
                own[u, :, cols] = part[96:]
            exchange(u).start()

        @pl.when(u >= LAG)
        def _():
            w = u - LAG
            exchange(w).wait_recv()
            for t in range(2):
                for v in range(2):
                    rows = slice(t * 32 + v * 16, t * 32 + v * 16 + 16)
                    done[w, t, 0, v] = (own[w, rows, :] + take[w, rows, :].astype(F32)).astype(BF)
            for v in range(2):
                rows = slice(64 + v * 16, 64 + v * 16 + 16)
                total = own[w, rows, :] + take[w, rows, :].astype(F32)
                for t in range(2):
                    mask = jnp.broadcast_to(wts[c, 24 + t:25 + t, 0:1], (16, 1))
                    done[w, t, 1, v] = (total * mask).astype(BF)
            for v in range(2):
                put_partner(w, v, c).start()
                put_own(w, v).start()

    send_b.wait_send()
    send_w.wait_send()
    ag_y.wait_send()
    for i in range(4):
        send_r(i, c).wait_send()
    for v in range(2):
        for r in (1, 2, 3):
            ag_to_first(r, v).wait_send()

    @pl.loop(0, 4)
    def _(u):
        for v in range(2):
            for r in (1, 2, 3):
                ag_to_second(u, v, r).wait_send()

    @pl.loop(0, 16)
    def _(u):
        exchange(u).wait_send()
        for v in range(2):
            put_partner(u, v, c).wait_send()
            put_partner(u, v, 1 - c).wait_recv()
            put_own(u, v).wait()


def shards(broadcast_ops, resident_ops, integrals, owner_list):
    weights = integrals[0, 0]
    owners = owner_list[0]
    pairs = jnp.arange(4)
    rank = jnp.sum(((owners[:, None] == owners[None, :]) & (pairs[:, None] < pairs[None, :])).astype(jnp.int32), axis=0)
    half = lax.axis_index("sector") // 2
    slots = []
    for h in (1 - half, half):
        slots.append((owners == 2 * h) & (rank == 0))
        slots.append((owners == 2 * h + 1) & (rank == 0))
        slots.append((owners // 2 == h) & (rank == 1))
    select = jnp.stack(slots)
    slot_weights = jnp.sum(jnp.where(select[:, :, None], weights[None], 0.0), axis=1)
    masks = jnp.stack([jnp.any((owners == 2 * half + t) & (rank == 1)) for t in range(2)]).astype(F32)
    table = jnp.concatenate([slot_weights.reshape(24), masks, jnp.zeros((6,), F32)])
    table = jnp.broadcast_to(table[:, None], (32, 128))
    hbm = pl.BlockSpec(memory_space=pl.ANY)
    dma = pltpu.SemaphoreType.DMA
    result = pl.pallas_call(
        kernel,
        out_shape=jax.ShapeDtypeStruct((2, 1024, 1024), BF),
        in_specs=[hbm, hbm, hbm],
        out_specs=hbm,
        scratch_shapes=[
            pltpu.VMEM((4, 32, 1024), F32),
            pltpu.VMEM((1024, 1024), F32),
            pltpu.VMEM((4, 16, 1024), BF),
            pltpu.VMEM((16, 2, 2, 4, 16, 1024), BF),
            pltpu.VMEM((2048, 1024), BF),
            pltpu.VMEM((2, 32, 128), F32),
            pltpu.VMEM((192, 2048), BF),
            pltpu.VMEM((16, 96, 1024), BF),
            pltpu.VMEM((16, 96, 1024), BF),
            pltpu.VMEM((16, 96, 1024), F32),
            pltpu.VMEM((16, 2, 2, 2, 16, 1024), BF),
            dma((6,)), dma((2,)), dma((1,)), dma((4,)), dma((4,)), dma((31,)), dma((32,)), dma((16,)), dma((16,)),
            dma((32,)), dma((32,)), dma((32,)),
        ],
        compiler_params=pltpu.CompilerParams(
            collective_id=0, has_side_effects=True, vmem_limit_bytes=56 * 2**20
        ),
    )(broadcast_ops[0], resident_ops[0, 0], table)
    return result.astype(F32)[None, None]


def solution(mesh):
    in_specs = (
        P("sector", None, "owner", None),
        P("sector", "owner", None, None),
        P("sector", "owner", None, None),
        P("owner", None),
    )
    out_specs = P("sector", "owner", None, None, None)
    return jax.shard_map(shards, mesh=mesh, in_specs=in_specs, out_specs=out_specs, check_vma=False)
```

time: 435 us -> 113 us (0.26)
  waiting for transfers between devices: 330 us -> 0 us
  Pallas kernels: 0 us -> 100 us
  matrix products: 83.2 us -> 0 us
  between operations: 13.4 us -> 0.02 us
  other arithmetic: 1.88 us -> 11.8 us
  local copies, waits for them, and re-layouts: 6.59 us -> 1 us
    psum x1 -> x0, waiting for transfers between devices: 181 us -> none  [shards(): lax.psum(partial_ops.astype(jnp.bfloat16), 'sector').astype(jnp.float32)]
    all_gather x1 -> x0, waiting for transfers between devices: 149 us -> none  [shards(): lax.all_gather(shared.astype(jnp.bfloat16), 'owner', axis=1, tiled=True)]
    pallas_call x0 -> x1, Pallas kernels: none -> 100 us  [shards(): pl.pallas_call(kernel, out_shape=jax.ShapeDtypeStruct((2, 1024, 1024), BF...]
    dot_general x3 -> x0, matrix products: 83.2 us -> none  [the longest x1 44.7 us: shards(): jnp.einsum('pk,kmn->pmn', weights, products, precision=highest)]
    broadcast_in_dim x0 -> x1, other arithmetic: none -> 6.64 us  [shards(): return result.astype(F32)[None, None]]
    broadcast_in_dim x1, local copies, waits for them, and re-layouts: 5.96 us -> 0.68 us  [shards(): table = jnp.broadcast_to(table[:, None], (32, 128))]
  transfers between devices with their start and end apart: 2 -> 0, of which waited for: 2 -> 0; matrix products, arithmetic and copies ran while one was open for 0% -> 0% of each run, Pallas kernels for 0% -> 0%
where the time goes in v1:
time: 113 us
  Pallas kernels  100 us (88%)
  other arithmetic  11.8 us (10%)
    pallas_call x1, Pallas kernels, shards(): pl.pallas_call(kernel, out_shape=jax.ShapeDtypeStruct((2, 1024, 1024), BF...  100 us
    broadcast_in_dim x1, other arithmetic, shards(): return result.astype(F32)[None, None]  6.64 us

profile of v1, /device:TPU:1, one launch (start us, length us, event | category | flops | bytes accessed | tf_op | source)
XLA Modules:
  0.0 113.0 jit_solution(14999704372949746804)
XLA Ops:
  0.0 0.8 convert_reduce_fusion
  0.8 1.4 %and_reduce_fusion.1 = (pred[]{:T(512)}, pred[]{:T(512)}) fusion(s32[]{:T(128)S(6)} %mul.5, s32[1,4]{1,0:T(1,128)} %param.7, s32[4]{0:T(128)S(1)} %convert_reduce_fusion, s32[]{:T(128)S(6)} %add.12), kind=kLoop, calls=%fused_computation.13 | loop fusion | flops 26 | bytes 42 | tf_op jit(solution)/shard_map/reduce_or | solution.py:220
  2.2 1.4 %add_convert_fusion = f32[2]{0:T(128)S(1)} fusion(pred[1]{0:T(512)(128)(4,1)} %bitcast.7, pred[1]{0:T(512)(128)(4,1)} %bitcast.6), kind=kLoop, calls=%fused_computation.5 | loop fusion | flops 4 | bytes 10 | tf_op jit(solution)/shard_map/convert_element_type | solution.py:220
  3.6 0.7 bitcast_and_fusion
  4.3 0.1 copy.5
  4.4 0.8 select_reduce_fusion
  5.2 0.1 copy.6
  5.3 0.1 reshape.29
  5.4 0.1 pad_maximum_fusion
  5.5 0.7 broadcast_in_dim.41.wt_hbm
  6.1 100.3 %shard_map.46 = bf16[2,1024,1024]{2,1,0:T(8,128)(2,1)} custom-call(f32[4,32,1024]{2,1,0:T(8,128)} %bitcast.20, f32[1024,1024]{1,0:T(8,128)} %bitcast.19, f32[32,128]{1,0:T(8,128)} %broadcast_in_dim.41.wt_hbm), custom_call_target="tpu_custom_call" | custom-call | tf_op jit(solution)/shard_map/pallas_call | solution.py:225
  106.4 6.6 %bitcast_convert_fusion = f32[1,1,2,1024,1024]{4,3,2,1,0:T(8,128)} fusion(bf16[2,1024,1024]{2,1,0:T(8,128)(2,1)} %shard_map.46), kind=kLoop, calls=%fused_computation | loop fusion | flops 2097152 | bytes 12582912 | tf_op jit(solution)/shard_map/broadcast_in_dim | solution.py:249
  (3 shorter events, 0.0 us)

commit v2 on v0

v2 whole, which is shorter than its diff:
```python
import jax
import jax.numpy as jnp
from jax import lax
from jax.experimental import pallas as pl
from jax.experimental.pallas import tpu as pltpu
from jax.sharding import PartitionSpec as P

MESH = pl.DeviceIdType.MESH
BF = jnp.bfloat16
F32 = jnp.float32
STEPS = 32
LAG = 9


def coords():
    s = lax.axis_index("sector")
    o = lax.axis_index("owner")
    return o // 8, lax.rem(o // 4, 2), lax.rem(o, 4), s // 2, lax.rem(s, 2)


def device(x, yl, z, yh, c):
    return (yh * 2 + c, lax.rem(x, 4) * 8 + yl * 4 + lax.rem(z, 4))


ORDER = (
    [(0, 0, 0), (1, 0, 0), (3, 0, 0), (0, 1, 0), (0, 3, 0), (0, 0, 1)]
    + [(1, 1, 0), (1, 3, 0), (3, 1, 0), (3, 3, 0), (1, 0, 1), (3, 0, 1), (0, 1, 1), (0, 3, 1), (2, 0, 0), (0, 2, 0)]
    + [(1, 1, 1), (1, 3, 1), (3, 1, 1), (3, 3, 1), (1, 2, 0), (3, 2, 0), (2, 1, 0), (2, 3, 0), (2, 0, 1), (0, 2, 1)]
    + [(1, 2, 1), (3, 2, 1), (2, 1, 1), (2, 3, 1), (2, 2, 0), (2, 2, 1)]
)
STEP = {at: i for i, at in enumerate(ORDER)}
SENDS = {
    1: [(2, 1, 0, 1), (2, 1, 0, 3)],
    2: [(2, 3, 0, 1), (2, 3, 0, 3)],
    5: [(1, 0, 1, 1), (1, 0, 1, 3), (2, 0, 1, 1), (2, 0, 1, 3)],
    6: [(1, 0, 0, 2), (2, 0, 0, 2)],
    10: [(2, 1, 1, 1), (2, 1, 1, 3)],
    11: [(2, 3, 1, 1), (2, 3, 1, 3)],
    12: [(2, 1, 0, 2), (2, 3, 0, 2)],
    14: [(2, 2, 0, 1), (2, 2, 0, 3)],
    15: [(1, 0, 1, 2), (2, 0, 1, 2)],
    17: [(2, 1, 1, 2), (2, 3, 1, 2)],
    18: [(2, 2, 0, 2)],
    24: [(2, 2, 1, 1), (2, 2, 1, 3)],
    25: [(2, 2, 1, 2)],
}
FIRST_SENDS = [(1, 0, 0, 1), (1, 0, 0, 3), (2, 0, 0, 1), (2, 0, 0, 3)]
ALL_SENDS = FIRST_SENDS + [send for sends in SENDS.values() for send in sends]


def parts(i):
    if isinstance(i, int):
        return ORDER[i]
    codes = [r1 + 4 * r2 + 16 * v for r1, r2, v in ORDER]
    code = codes[0]
    for n in range(1, STEPS):
        code = code + lax.div(i + (STEPS - n), STEPS) * (codes[n] - codes[n - 1])
    return lax.rem(code, 4), lax.rem(lax.div(code, 4), 4), lax.div(code, 16)


def kernel(b_hbm, r_hbm, w_hbm, o_hbm, out, bf32, rf32, bst, ops, res, table, owners, wts, wide, give, take, own, done,
           load_sem, pair_send, pair_recv, res_send, res_recv, ag_send, ag_recv, ex_send, ex_recv, fin_send, fin_recv):
    x, yl, z, yh, c = coords()
    partner = device(x, yl, z, yh, 1 - c)
    y_near = device(x, 1 - yl, z, yh, c)
    y_far = device(x, yl, z, 1 - yh, c)

    def first(r):
        return device(x + (4 - r) * (1 - c), yl, z + (4 - r) * c, yh, c)

    def second(r):
        return device(x + (4 - r) * c, yl, z + (4 - r) * (1 - c), yh, c)

    def rows_of(i, core):
        r1, r2, v = parts(i)
        xs = lax.rem(x + r1 * (1 - core) + r2 * core, 4)
        zs = lax.rem(z + r1 * core + r2 * (1 - core), 4)
        ys = yl * (1 - v) + (1 - yl) * v
        return pl.ds(pl.multiple_of((xs * 8 + ys * 4 + zs) * 32 + core * 16, 16), 16)

    def remote(src, dst, ssem, rsem, dev):
        return pltpu.make_async_remote_copy(
            src_ref=src, dst_ref=dst, send_sem=ssem, recv_sem=rsem, device_id=dev, device_id_type=MESH
        )

    load_b = pltpu.make_async_copy(b_hbm, bf32, load_sem.at[0])
    load_b.start()
    load_w = pltpu.make_async_copy(w_hbm, table, load_sem.at[1])
    load_w.start()
    load_o = pltpu.make_async_copy(o_hbm, owners, load_sem.at[2])
    load_o.start()

    def load_r(i):
        part = pl.ds(i * 256, 256)
        return pltpu.make_async_copy(r_hbm.at[part], rf32.at[part], load_sem.at[3 + i])

    for i in range(4):
        load_r(i).start()

    barrier = pltpu.get_barrier_semaphore()
    peers = [partner, y_near, y_far] + [first(r) for r in (1, 2, 3)] + [second(r) for r in (1, 2, 3)]
    for peer in peers:
        pl.semaphore_signal(barrier, inc=1, device_id=peer, device_id_type=MESH)

    load_b.wait()
    mine = pl.ds(pl.multiple_of(c * 16, 16), 16)
    theirs = pl.ds(pl.multiple_of((1 - c) * 16, 16), 16)
    for k in range(4):
        bst[k] = bf32[k, theirs, :].astype(BF)
    for k in range(4):
        ops[0, c, k] = bf32[k, mine, :].astype(BF)

    load_w.wait()
    load_o.wait()
    owner = [owners[p] for p in range(4)]
    one, zero = jnp.float32(1), jnp.float32(0)
    twice = [sum([(jnp.where(owner[q] == owner[p], one, zero)) for q in range(p)], zero) for p in range(4)]
    row = 0
    for half in (1 - yh, yh):
        for t in range(3):
            if t < 2:
                pick = [jnp.where(owner[p] == 2 * half + t, one, zero) * (one - twice[p]) for p in range(4)]
            else:
                pick = [jnp.where(owner[p] // 2 == half, one, zero) * twice[p] for p in range(4)]
            for k in range(4):
                value = (pick[0] * table[0, k] + pick[1] * table[1, k]) + (pick[2] * table[2, k] + pick[3] * table[3, k])
                wts[c, row:row + 1, :] = jnp.full((1, 128), value, F32)
                row += 1
    for t in range(2):
        flag = sum([jnp.where(owner[p] == 2 * yh + t, one, zero) * twice[p] for p in range(4)], zero)
        wts[c, 24 + t:25 + t, :] = jnp.full((1, 128), flag, F32)

    pl.semaphore_wait(barrier, len(peers))
    send_b = remote(bst, ops.at[0, c], pair_send.at[0], ag_recv.at[0], partner)
    send_b.start()
    send_w = remote(wts.at[c], wts.at[c], pair_send.at[1], pair_recv.at[0], partner)
    send_w.start()

    def gather(send):
        axis, r1, v, r = send
        to, dev = (STEP[r, 0, v], first(r)) if axis == 1 else (STEP[r1, r, v], second(r))
        return remote(ops.at[STEP[r1, 0, v]], ops.at[to], ag_send.at[ALL_SENDS.index(send)], ag_recv.at[to], dev)

    def arrived(i):
        remote(ops.at[i], ops.at[i], ag_send.at[0], ag_recv.at[i], partner).wait_recv()

    def send_r(i, core):
        part = pl.ds(pl.multiple_of(core * 1024 + i * 256, 256), 256)
        return remote(res.at[part], res.at[part], res_send.at[i], res_recv.at[i], partner)

    def put_r(i):
        load_r(i).wait()
        res[pl.ds(pl.multiple_of(c * 1024 + i * 256, 256), 256), :] = rf32[i * 256:(i + 1) * 256, :].astype(BF)
        send_r(i, c).start()

    def ag_y(core, n):
        return remote(ops.at[0, core], ops.at[5, core], ag_send.at[30 + n], ag_recv.at[5 + 27 * n], y_near)

    ag_y(c, 0).start()
    put_r(0)
    remote(bst, ops.at[0, 1 - c], pair_send.at[0], ag_recv.at[0], partner).wait_recv()
    ag_y(1 - c, 1).start()
    for send in FIRST_SENDS:
        gather(send).start()
    for i in range(1, 4):
        put_r(i)

    remote(wts.at[1 - c], wts.at[1 - c], pair_send.at[1], pair_recv.at[0], partner).wait_recv()
    for i in range(4):
        send_r(i, 1 - c).wait_recv()

    def exchange(i):
        return remote(give.at[i], take.at[i], ex_send.at[i], ex_recv.at[i], y_far)

    def put_partner(i, rows):
        return remote(done.at[i], out.at[:, rows, :], fin_send.at[i], fin_recv.at[i], partner)

    @pl.loop(0, STEPS + LAG)
    def _(i):
        @pl.when(i < STEPS)
        def _():
            @pl.when(((i > 0) & (i < 5)) | (i > 5))
            def _():
                arrived(i)

            @pl.when(i == 5)
            def _():
                ag_y(c, 0).wait_recv()
                ag_y(1 - c, 1).wait_recv()

            for step, sends in SENDS.items():
                @pl.when(i == step)
                def _():
                    for send in sends:
                        gather(send).start()

            for s in range(2):
                for half in range(2):
                    lanes = [slice(half * 512 + n * 128, half * 512 + (n + 1) * 128) for n in range(4)]
                    b = [[ops[i, s, k, :, lane].astype(F32) for lane in lanes] for k in range(4)]
                    for t in range(6):
                        w = [jnp.broadcast_to(wts[s, t * 4 + k:t * 4 + k + 1, :], (16, 128)) for k in range(4)]
                        for n in range(4):
                            acc = (b[0][n] * w[0] + b[1][n] * w[1]) + (b[2][n] * w[2] + b[3][n] * w[3])
                            col = s * 1024 + half * 512 + n * 128
                            wide[t * 16:t * 16 + 16, col:col + 128] = acc.astype(BF)
            for n in range(4):
                cols = slice(n * 256, (n + 1) * 256)
                part = jnp.dot(wide[...], res[:, cols], preferred_element_type=F32)
                give[i, :, cols] = part[:48].astype(BF)
                own[i, :, cols] = part[48:]
            exchange(i).start()

        @pl.when(i >= LAG)
        def _():
            w = i - LAG
            exchange(w).wait_recv()
            firsts = [own[w, t * 16:t * 16 + 16, :] + take[w, t * 16:t * 16 + 16, :].astype(F32) for t in range(2)]
            extra = own[w, 32:48, :] + take[w, 32:48, :].astype(F32)
            mask = [jnp.broadcast_to(wts[c, 24 + t:25 + t, 0:1], (16, 1)) for t in range(2)]
            even = lax.rem(c + 1, 2).astype(F32)
            odd = c.astype(F32)
            done[w, 0] = (firsts[0] * odd + firsts[1] * even)
            done[w, 1] = (extra * (mask[0] * odd + mask[1] * even))
            rows = rows_of(w, c)
            put_partner(w, rows).start()
            out[0, rows, :] = (firsts[0] * even + firsts[1] * odd)
            out[1, rows, :] = (extra * (mask[0] * even + mask[1] * odd))

    send_b.wait_send()
    send_w.wait_send()
    ag_y(c, 0).wait_send()
    ag_y(1 - c, 1).wait_send()
    for i in range(4):
        send_r(i, c).wait_send()
    for send in ALL_SENDS:
        gather(send).wait_send()

    @pl.loop(0, STEPS)
    def _(i):
        exchange(i).wait_send()

    for i in range(STEPS):
        put_partner(i, rows_of(i, c)).wait_send()
        put_partner(i, rows_of(i, 1 - c)).wait_recv()


def shards(broadcast_ops, resident_ops, integrals, owner_list):
    hbm = pl.BlockSpec(memory_space=pltpu.HBM)
    dma = pltpu.SemaphoreType.DMA
    result = pl.pallas_call(
        kernel,
        out_shape=OUT,
        in_specs=[hbm, hbm, hbm, hbm],
        out_specs=pl.BlockSpec(memory_space=pltpu.VMEM),
        scratch_shapes=[
            pltpu.VMEM((4, 32, 1024), F32),
            pltpu.VMEM((1024, 1024), F32),
            pltpu.VMEM((4, 16, 1024), BF),
            pltpu.VMEM((STEPS, 2, 4, 16, 1024), BF),
            pltpu.VMEM((2048, 1024), BF),
            pltpu.SMEM((4, 4), F32),
            pltpu.SMEM((4,), jnp.int32),
            pltpu.VMEM((2, 32, 128), F32),
            pltpu.VMEM((96, 2048), BF),
            pltpu.VMEM((STEPS, 48, 1024), BF),
            pltpu.VMEM((STEPS, 48, 1024), BF),
            pltpu.VMEM((STEPS, 48, 1024), F32),
            pltpu.VMEM((STEPS, 2, 16, 1024), F32),
            dma((7,)), dma((2,)), dma((1,)), dma((4,)), dma((4,)), dma((32,)), dma((STEPS + 1,)), dma((STEPS,)),
            dma((STEPS,)), dma((STEPS,)), dma((STEPS,)),
        ],
        compiler_params=pltpu.CompilerParams(
            collective_id=0, has_side_effects=True, vmem_limit_bytes=67043328 - 8388608
        ),
    )(broadcast_ops[0], resident_ops[0, 0], integrals[0, 0], owner_list[0])
    return result[None, None]


OUT = pltpu.VMEM((2, 1024, 1024), F32)


def solution(mesh):
    in_specs = (
        P("sector", None, "owner", None),
        P("sector", "owner", None, None),
        P("sector", "owner", None, None),
        P("owner", None),
    )
    out_specs = P("sector", "owner", None, None, None)
    return jax.shard_map(shards, mesh=mesh, in_specs=in_specs, out_specs=out_specs, check_vma=False)
```

time: 435 us -> 90.7 us (0.21)
  waiting for transfers between devices: 330 us -> 0 us
  Pallas kernels: 0 us -> 87.2 us
  matrix products: 83.2 us -> 0 us
  between operations: 13.4 us -> 0.01 us
    psum x1 -> x0, waiting for transfers between devices: 181 us -> none  [shards(): lax.psum(partial_ops.astype(jnp.bfloat16), 'sector').astype(jnp.float32)]
    all_gather x1 -> x0, waiting for transfers between devices: 149 us -> none  [shards(): lax.all_gather(shared.astype(jnp.bfloat16), 'owner', axis=1, tiled=True)]
    pallas_call x0 -> x1, Pallas kernels: none -> 87.2 us  [shards(): pl.pallas_call(kernel, out_shape=OUT, in_specs=[hbm, hbm, hbm, hbm], out_...]
    dot_general x3 -> x0, matrix products: 83.2 us -> none  [the longest x1 44.7 us: shards(): jnp.einsum('pk,kmn->pmn', weights, products, precision=highest)]
    broadcast_in_dim x1 -> x0, local copies, waits for them, and re-layouts: 5.96 us -> none  [shards(): return result[None, None]]
  transfers between devices with their start and end apart: 2 -> 0, of which waited for: 2 -> 0; matrix products, arithmetic and copies ran while one was open for 0% -> 0% of each run, Pallas kernels for 0% -> 0%
where the time goes in v2:
time: 90.7 us; the launch traced here: 90.6 us
  Pallas kernels  87.2 us (96%)
  local copies, waits for them, and re-layouts  3.4 us (4%)
    pallas_call x1, Pallas kernels, shards(): pl.pallas_call(kernel, out_shape=OUT, in_specs=[hbm, hbm, hbm, hbm], out_...  87.2 us
    unnamed x1, local copies, waits for them, and re-layouts  3.4 us

profile of v2, /device:TPU:1, one launch (start us, length us, event | category | flops | bytes accessed | tf_op | source)
XLA Modules:
  0.0 90.6 jit_solution(17062136353136546247)
XLA Ops:
  0.0 87.2 %shard_map.46 = f32[2,1024,1024]{2,1,0:T(8,128)S(1)} custom-call(f32[4,32,1024]{2,1,0:T(8,128)} %bitcast.7, f32[1024,1024]{1,0:T(8,128)} %bitcast.6, f32[4,4]{1,0:T(4,128)} %bitcast.8, s32[4]{0:T(128)} %bitcast.9), custom_call_target="tpu_custom_call" | custom-call | tf_op jit(solution)/shard_map/pallas_call | solution.py:251
  87.2 3.4 %copy.6 = f32[1,1,2,1024,1024]{4,3,2,1,0:T(8,128)} copy(f32[1,1,2,1024,1024]{4,3,2,1,0:T(8,128)S(1)} %bitcast.5) | data formatting | bytes 16777216

commit v3 on v2

--- a/solution.py
+++ b/solution.py
@@ -30,6 +30,7 @@
 )
 STEP = {at: i for i, at in enumerate(ORDER)}
 SENDS = {
+    0: [(2, 0, 0, 1), (2, 0, 0, 3)],
     1: [(2, 1, 0, 1), (2, 1, 0, 3)],
     2: [(2, 3, 0, 1), (2, 3, 0, 3)],
     5: [(1, 0, 1, 1), (1, 0, 1, 3), (2, 0, 1, 1), (2, 0, 1, 3)],
@@ -44,7 +45,7 @@
     24: [(2, 2, 1, 1), (2, 2, 1, 3)],
     25: [(2, 2, 1, 2)],
 }
-FIRST_SENDS = [(1, 0, 0, 1), (1, 0, 0, 3), (2, 0, 0, 1), (2, 0, 0, 3)]
+FIRST_SENDS = [(1, 0, 0, 1), (1, 0, 0, 3)]
 ALL_SENDS = FIRST_SENDS + [send for sends in SENDS.values() for send in sends]
 
 
@@ -130,6 +131,10 @@
         flag = sum([jnp.where(owner[p] == 2 * yh + t, one, zero) * twice[p] for p in range(4)], zero)
         wts[c, 24 + t:25 + t, :] = jnp.full((1, 128), flag, F32)
 
+    for i in range(4):
+        load_r(i).wait()
+        res[pl.ds(pl.multiple_of(c * 1024 + i * 256, 256), 256), :] = rf32[i * 256:(i + 1) * 256, :].astype(BF)
+
     pl.semaphore_wait(barrier, len(peers))
     send_b = remote(bst, ops.at[0, c], pair_send.at[0], ag_recv.at[0], partner)
     send_b.start()
@@ -148,22 +153,16 @@
         part = pl.ds(pl.multiple_of(core * 1024 + i * 256, 256), 256)
         return remote(res.at[part], res.at[part], res_send.at[i], res_recv.at[i], partner)
 
-    def put_r(i):
-        load_r(i).wait()
-        res[pl.ds(pl.multiple_of(c * 1024 + i * 256, 256), 256), :] = rf32[i * 256:(i + 1) * 256, :].astype(BF)
-        send_r(i, c).start()
-
     def ag_y(core, n):
         return remote(ops.at[0, core], ops.at[5, core], ag_send.at[30 + n], ag_recv.at[5 + 27 * n], y_near)
 
     ag_y(c, 0).start()
-    put_r(0)
+    for i in range(4):
+        send_r(i, c).start()
     remote(bst, ops.at[0, 1 - c], pair_send.at[0], ag_recv.at[0], partner).wait_recv()
     ag_y(1 - c, 1).start()
     for send in FIRST_SENDS:
         gather(send).start()
-    for i in range(1, 4):
-        put_r(i)
 
     remote(wts.at[1 - c], wts.at[1 - c], pair_send.at[1], pair_recv.at[0], partner).wait_recv()
     for i in range(4):

time: 90.7 us -> 88.5 us (0.976)
  Pallas kernels: 87.2 us -> 85 us
    pallas_call x1, Pallas kernels: 87.2 us -> 85 us  [shards(): pl.pallas_call(kernel, out_shape=OUT, in_specs=[hbm, hbm, hbm, hbm], out_...]
where the time goes in v3:
time: 88.5 us; the launch traced here: 88.4 us
  Pallas kernels  85 us (96%)
  local copies, waits for them, and re-layouts  3.4 us (4%)
    pallas_call x1, Pallas kernels, shards(): pl.pallas_call(kernel, out_shape=OUT, in_specs=[hbm, hbm, hbm, hbm], out_...  85 us
    unnamed x1, local copies, waits for them, and re-layouts  3.4 us

profile of v3, /device:TPU:1, one launch (start us, length us, event | category | flops | bytes accessed | tf_op | source)
XLA Modules:
  0.0 88.4 jit_solution(6115246595033411079)
XLA Ops:
  0.0 85.0 %shard_map.46 = f32[2,1024,1024]{2,1,0:T(8,128)S(1)} custom-call(f32[4,32,1024]{2,1,0:T(8,128)} %bitcast.7, f32[1024,1024]{1,0:T(8,128)} %bitcast.6, f32[4,4]{1,0:T(4,128)} %bitcast.8, s32[4]{0:T(128)} %bitcast.9), custom_call_target="tpu_custom_call" | custom-call | tf_op jit(solution)/shard_map/pallas_call | solution.py:250
  85.0 3.4 %copy.6 = f32[1,1,2,1024,1024]{4,3,2,1,0:T(8,128)} copy(f32[1,1,2,1024,1024]{4,3,2,1,0:T(8,128)S(1)} %bitcast.5) | data formatting | bytes 16777216

commit v4 on v3

--- a/solution.py
+++ b/solution.py
@@ -23,7 +23,7 @@
 
 
 ORDER = (
-    [(0, 0, 0), (1, 0, 0), (3, 0, 0), (0, 1, 0), (0, 3, 0), (0, 0, 1)]
+    [(0, 0, 0), (1, 0, 0), (3, 0, 0), (0, 0, 1), (0, 1, 0), (0, 3, 0)]
     + [(1, 1, 0), (1, 3, 0), (3, 1, 0), (3, 3, 0), (1, 0, 1), (3, 0, 1), (0, 1, 1), (0, 3, 1), (2, 0, 0), (0, 2, 0)]
     + [(1, 1, 1), (1, 3, 1), (3, 1, 1), (3, 3, 1), (1, 2, 0), (3, 2, 0), (2, 1, 0), (2, 3, 0), (2, 0, 1), (0, 2, 1)]
     + [(1, 2, 1), (3, 2, 1), (2, 1, 1), (2, 3, 1), (2, 2, 0), (2, 2, 1)]
@@ -33,7 +33,7 @@
     0: [(2, 0, 0, 1), (2, 0, 0, 3)],
     1: [(2, 1, 0, 1), (2, 1, 0, 3)],
     2: [(2, 3, 0, 1), (2, 3, 0, 3)],
-    5: [(1, 0, 1, 1), (1, 0, 1, 3), (2, 0, 1, 1), (2, 0, 1, 3)],
+    3: [(1, 0, 1, 1), (1, 0, 1, 3), (2, 0, 1, 1), (2, 0, 1, 3)],
     6: [(1, 0, 0, 2), (2, 0, 0, 2)],
     10: [(2, 1, 1, 1), (2, 1, 1, 3)],
     11: [(2, 3, 1, 1), (2, 3, 1, 3)],
@@ -154,15 +154,22 @@
         return remote(res.at[part], res.at[part], res_send.at[i], res_recv.at[i], partner)
 
     def ag_y(core, n):
-        return remote(ops.at[0, core], ops.at[5, core], ag_send.at[30 + n], ag_recv.at[5 + 27 * n], y_near)
+        return remote(ops.at[0, core], ops.at[3, core], ag_send.at[30 + n], ag_recv.at[3 + 32 * n], y_near)
+
+    def near(r, core, n):
+        to = STEP[r, 0, 0]
+        return remote(ops.at[0, core], ops.at[to, core], ag_send.at[32 + r // 2 + 2 * n],
+                      ag_recv.at[to + 32 * n], first(r))
 
     ag_y(c, 0).start()
+    for r in (1, 3):
+        near(r, c, 0).start()
     for i in range(4):
         send_r(i, c).start()
     remote(bst, ops.at[0, 1 - c], pair_send.at[0], ag_recv.at[0], partner).wait_recv()
     ag_y(1 - c, 1).start()
-    for send in FIRST_SENDS:
-        gather(send).start()
+    for r in (1, 3):
+        near(r, 1 - c, 1).start()
 
     remote(wts.at[1 - c], wts.at[1 - c], pair_send.at[1], pair_recv.at[0], partner).wait_recv()
     for i in range(4):
@@ -178,11 +185,17 @@
     def _(i):
         @pl.when(i < STEPS)
         def _():
-            @pl.when(((i > 0) & (i < 5)) | (i > 5))
+            @pl.when(i > 3)
             def _():
                 arrived(i)
 
-            @pl.when(i == 5)
+            for r in (1, 3):
+                @pl.when(i == STEP[r, 0, 0])
+                def _():
+                    near(r, c, 0).wait_recv()
+                    near(r, 1 - c, 1).wait_recv()
+
+            @pl.when(i == 3)
             def _():
                 ag_y(c, 0).wait_recv()
                 ag_y(1 - c, 1).wait_recv()
@@ -232,8 +245,11 @@
     ag_y(1 - c, 1).wait_send()
     for i in range(4):
         send_r(i, c).wait_send()
-    for send in ALL_SENDS:
+    for send in ALL_SENDS[len(FIRST_SENDS):]:
         gather(send).wait_send()
+    for r in (1, 3):
+        near(r, c, 0).wait_send()
+        near(r, 1 - c, 1).wait_send()
 
     @pl.loop(0, STEPS)
     def _(i):
@@ -266,7 +282,7 @@
             pltpu.VMEM((STEPS, 48, 1024), BF),
             pltpu.VMEM((STEPS, 48, 1024), F32),
             pltpu.VMEM((STEPS, 2, 16, 1024), F32),
-            dma((7,)), dma((2,)), dma((1,)), dma((4,)), dma((4,)), dma((32,)), dma((STEPS + 1,)), dma((STEPS,)),
+            dma((7,)), dma((2,)), dma((1,)), dma((4,)), dma((4,)), dma((36,)), dma((STEPS + 4,)), dma((STEPS,)),
             dma((STEPS,)), dma((STEPS,)), dma((STEPS,)),
         ],
         compiler_params=pltpu.CompilerParams(

time: 88.5 us -> 88.6 us (level)
  no operation moved by 1% of the time
where the time goes in v4:
time: 88.6 us; the launch traced here: 88.5 us
  Pallas kernels  85.1 us (96%)
  local copies, waits for them, and re-layouts  3.4 us (4%)
    pallas_call x1, Pallas kernels, shards(): pl.pallas_call(kernel, out_shape=OUT, in_specs=[hbm, hbm, hbm, hbm], out_...  85.1 us
    unnamed x1, local copies, waits for them, and re-layouts  3.4 us

profile of v4, /device:TPU:1, one launch (start us, length us, event | category | flops | bytes accessed | tf_op | source)
XLA Modules:
  0.0 88.5 jit_solution(320754171149011810)
XLA Ops:
  0.0 85.1 %shard_map.46 = f32[2,1024,1024]{2,1,0:T(8,128)S(1)} custom-call(f32[4,32,1024]{2,1,0:T(8,128)} %bitcast.7, f32[1024,1024]{1,0:T(8,128)} %bitcast.6, f32[4,4]{1,0:T(4,128)} %bitcast.8, s32[4]{0:T(128)} %bitcast.9), custom_call_target="tpu_custom_call" | custom-call | tf_op jit(solution)/shard_map/pallas_call | solution.py:266
  85.1 3.4 %copy.6 = f32[1,1,2,1024,1024]{4,3,2,1,0:T(8,128)} copy(f32[1,1,2,1024,1024]{4,3,2,1,0:T(8,128)S(1)} %bitcast.5) | data formatting | bytes 16777216
